TPU v7x, 256 devices: a whole 4x4x8 slice. The times are simulated.
256 devices in a mesh: gx: 4 (over z_hi), gy: 4 (over x), ha: 16 (over z_lo, y, core).
Axes of the slice: x: 4, y: 4, z: 8 (z_hi: 4, z_lo: 2; z = z_hi * 2 + z_lo), core: 2. Of those that a mesh axis runs over, the one named last changes fastest.
Arguments:
- wavefield: float32 [4, 4, 16, 32, 9, 512], P('gx', 'gy', 'ha'), may hold values from -6 to 6
- deriv_ops: float32 [3, 512, 512], replicated, may hold values from -0.25 to 0.25
- density: float32 [4, 4, 16, 32], P('gx', 'gy', 'ha'), may hold values from 1 to 3
- lame_first: float32 [4, 4, 16, 32], P('gx', 'gy', 'ha'), may hold values from 0.5 to 2
- shear_modulus: float32 [4, 4, 16, 32], P('gx', 'gy', 'ha'), may hold values from 0.3 to 1
- high_order: int32 [4, 4, 16, 32], P('gx', 'gy', 'ha'), may hold values from 0 to 1, as said below
- element_cell: int32 [4, 4, 16, 32], P('gx', 'gy', 'ha'), may hold values from 0 to 31, each once within a row
- face_orient: int32 [4, 4, 16, 6, 32], P('gx', 'gy', 'ha'), may hold values from 0 to 7
Outputs:
- advanced: float32 [4, 4, 16, 32, 9, 512], P('gx', 'gy', 'ha')
Inputs may be any that keep to these rules, and one draw needn't show every extreme that they name: `high_order`: within each group of devices along ha that share gx and gy, exactly half of the devices have 16 flagged elements and the others none; which devices and which elements are drawn. `element_cell`: on every device a permutation of the cells 0 to 31.
All inputs are finite; a program needn't handle non-finite values.
Results may differ from a plain program's by a relative error of at most 0.0001.
Values sent between devices are 32-bit elements; how exact they have to be, the bound alone decides.
A program may use at most 128 MiB of HBM per device.

v0:
```python
import math

import jax
import jax.numpy as jnp
from jax import lax
from jax.experimental import pallas as pl
from jax.experimental.pallas import tpu as pltpu
from jax.sharding import PartitionSpec as P

ELEMENTS = 32
FIELDS = 9
NODES = 512
STEPS = 2
DT_STEP = 0.8
LIFT_COEF = 2.0
X_FIELDS = (0, 1, 2, 3, 6, 8)
Y_FIELDS = (0, 1, 2, 6, 4, 7)
Z_FIELDS = (0, 1, 2, 8, 7, 5)
AXIS_FIELDS = (X_FIELDS, Y_FIELDS, Z_FIELDS)
MESH_AXES = ("gx", "gy", "ha")
SERIES = tuple(DT_STEP**k / math.factorial(k + 1) for k in range(6))
F32 = jnp.float32
BF16 = jnp.bfloat16
I32 = jnp.int32
NT = (((1,), (1,)), ((), ()))
HIGHEST = lax.Precision.HIGHEST


def dot(a, b):
    return jnp.dot(a, b, preferred_element_type=F32)


def halves(value):
    high = value.astype(BF16)
    return high, (value - high.astype(F32)).astype(BF16)


def thirds(value):
    high = value.astype(BF16)
    rest = value - high.astype(F32)
    mid = rest.astype(BF16)
    return high, mid, (rest - mid.astype(F32)).astype(BF16)


def rows_of(field):
    return slice(ELEMENTS * field, ELEMENTS * (field + 1))


def iota(shape, dim):
    return lax.broadcasted_iota(I32, shape, dim)


def face_node(column):
    face = column // 64
    p = (column // 8) % 8
    r = column % 8
    far = 7 * (face % 2)
    return jnp.where(face < 2, p * 64 + far * 8 + r, p * 64 + r * 8 + far)


def kernel(
    wave, dops, dens, lame, shear, hot, cell, orient, out,
    wf, wh, wl, small, coef, flags, index, q, acc, xh, xl, deriv, pick, lift, tr, ch, cl, cx,
    send_x, send_y, send_z, recv_x, recv_y, recv_z, load_sem, send_sem, recv_sem,
):
    barrier = pltpu.get_barrier_semaphore()
    place = [lax.axis_index(a) for a in MESH_AXES]
    count = [lax.axis_size(a) for a in MESH_AXES]
    up = [{a: lax.rem(i + 1, n)} for a, i, n in zip(MESH_AXES, place, count)]
    down = [{a: lax.rem(i + n - 1, n)} for a, i, n in zip(MESH_AXES, place, count)]
    for target in up + down:
        pl.semaphore_signal(barrier, 1, device_id=target, device_id_type=pl.DeviceIdType.MESH)

    loads = [pltpu.make_async_copy(dops.at[a], wf.at[a], load_sem.at[a]) for a in range(3)]
    for load in loads:
        load.start()

    small[...] = jnp.zeros_like(small)
    small[0:1, :] = dens[...]
    small[1:2, :] = lame[...]
    small[2:3, :] = shear[...]
    small[3:4, :] = hot[...].astype(F32)
    small[4:10, :] = orient[...].astype(F32)
    small[10:11, :] = cell[...].astype(F32)
    square = (ELEMENTS, ELEMENTS)
    place_cell = (iota(square, 0) == jnp.broadcast_to(cell[...], square)).astype(F32)
    by_cell = lax.dot_general(place_cell, small[...], NT, precision=HIGHEST)
    same = (iota(square, 0) == iota(square, 1)).astype(F32)
    by_element = lax.dot_general(same, small[...], NT, precision=HIGHEST)
    wide = (ELEMENTS, 128)
    inv_rho = 1.0 / by_cell[:, 0:1]
    lame_col = by_cell[:, 1:2]
    shear_col = by_cell[:, 2:3]
    coef[0] = jnp.broadcast_to(inv_rho, wide)
    coef[1] = jnp.broadcast_to(lame_col, wide)
    coef[2] = jnp.broadcast_to(shear_col, wide)
    coef[3] = jnp.broadcast_to(jnp.sqrt((lame_col + 2.0 * shear_col) * inv_rho), wide)
    flags[...] = jnp.broadcast_to(by_cell[:, 3:4], wide)
    lane = iota(wide, 1)
    p_pos = (lane // 8) % 8
    r_pos = lane % 8
    for d in range(3):
        low = jnp.broadcast_to(by_cell[:, 4 + 2 * d : 5 + 2 * d], wide)
        high = jnp.broadcast_to(by_cell[:, 5 + 2 * d : 6 + 2 * d], wide)
        code = jnp.where(lane < 64, low, high).astype(I32)
        p_src = jnp.where((code & 1) != 0, 7 - p_pos, p_pos)
        r_src = jnp.where((code & 2) != 0, 7 - r_pos, r_pos)
        node = jnp.where((code & 4) != 0, r_src * 8 + p_src, p_src * 8 + r_src)
        index[d] = node + jnp.where(lane < 64, 64, 0)
    pick[...] = (iota((NODES, 256), 0) == face_node(iota((NODES, 256), 1))).astype(BF16)
    lift[...] = (iota((256, NODES), 1) == face_node(iota((256, NODES), 0))).astype(BF16)
    gather_in = place_cell.astype(BF16)
    for f in range(FIELDS):
        a, b, c = thirds(wave[f])
        q[f] = dot(gather_in, a) + dot(gather_in, b) + dot(gather_in, c)

    for a in range(3):
        loads[a].wait()

        def split(i, carry, a=a):
            part = pl.ds(pl.multiple_of(i * 64, 64), 64)
            h, l = halves(wf[a, part, :])
            wh[a, part, :] = h
            wl[a, part, :] = l
            return carry

        lax.fori_loop(0, NODES // 64, split, 0)

    for recv, at, n in zip((recv_x, recv_y, recv_z), place, count):
        for edge, slot in ((0, 0), (n - 1, 1)):

            @pl.when(at == edge)
            def _(recv=recv, slot=slot):
                for s in range(STEPS):
                    recv[s, slot] = jnp.zeros_like(recv[s, slot])

    def set_operand(source):
        for f in range(FIELDS):
            xh[rows_of(f), :], xl[rows_of(f), :] = halves(source[f])

    def derive():
        for a, fields in enumerate(AXIS_FIELDS):
            h = jnp.concatenate([xh[rows_of(f), :] for f in fields], axis=0)
            l = jnp.concatenate([xl[rows_of(f), :] for f in fields], axis=0)
            deriv[a] = dot(h, wh[a]) + dot(l, wh[a]) + dot(h, wl[a])

    def rates(part):
        x = [deriv[0, rows_of(i), part] for i in range(6)]
        y = [deriv[1, rows_of(i), part] for i in range(6)]
        z = [deriv[2, rows_of(i), part] for i in range(6)]
        inv, lam, mu = coef[0], coef[1], coef[2]
        lam_div = lam * (x[0] + y[1] + z[2])
        mu2 = 2.0 * mu
        return [
            inv * (x[3] + y[3] + z[3]),
            inv * (x[4] + y[4] + z[4]),
            inv * (x[5] + y[5] + z[5]),
            lam_div + mu2 * x[0],
            lam_div + mu2 * y[1],
            lam_div + mu2 * z[2],
            mu * (x[1] + y[0]),
            mu * (y[2] + z[1]),
            mu * (x[2] + z[0]),
        ]

    def advance(first, weight, only_flagged):
        derive()
        for j in range(4):
            part = slice(128 * j, 128 * (j + 1))
            for f, rate in enumerate(rates(part)):
                term = weight * rate
                if only_flagged:
                    term = jnp.where(flags[...] > 0.5, term, 0.0)
                base = q if first else acc
                acc[f, :, part] = base[f, :, part] + term
                xh[rows_of(f), part], xl[rows_of(f), part] = halves(rate)

    def pack_pairs(tile, upper, dest):
        keep = (iota((8, 128), 1) >= 64) if upper else (iota((8, 128), 1) < 64)
        for f in range(4):
            dest[f] = jnp.where(keep, tile(f), pltpu.roll(tile(f + 5), 64, 1))
        dest[4] = tile(4)

    def unpack_pairs(source, f):
        return source[f] if f < 5 else pltpu.roll(source[f - 5], 64, 1)

    sub = iota((8, 128), 0)
    lo_lane = iota((8, 128), 1) < 64
    even = sub % 2 == 0

    def pack_rows_y(f, first_row):
        result = None
        for a in range(4):
            tile = tr[1, f, 8 * a : 8 * a + 8, :]
            shift = (2 * a - first_row) % 8
            moved = pltpu.roll(tile, shift, 0) if shift else tile
            result = moved if a == 0 else jnp.where(sub // 2 == a, moved, result)
        return result

    def pack_z(f, odd):
        strips = []
        for a in range(2):
            one = tr[2, f, 8 * a : 8 * a + 8, :]
            two = tr[2, f, 8 * a + 16 : 8 * a + 24, :]
            if odd:
                strips.append(jnp.where(even, pltpu.roll(two, 7, 0), one))
            else:
                strips.append(jnp.where(even, one, pltpu.roll(two, 1, 0)))
        keep = jnp.logical_not(lo_lane) if odd else lo_lane
        return jnp.where(keep, strips[0], pltpu.roll(strips[1], 64, 1))

    sends = (send_x, send_y, send_z)
    recvs = (recv_x, recv_y, recv_z)

    def copies(step):
        made = []
        for d in range(3):
            for way, target in ((0, up[d]), (1, down[d])):
                made.append(
                    pltpu.make_async_remote_copy(
                        src_ref=sends[d].at[way],
                        dst_ref=recvs[d].at[step, way],
                        send_sem=send_sem.at[step, 2 * d + way],
                        recv_sem=recv_sem.at[step, 2 * d + way],
                        device_id=target,
                        device_id_type=pl.DeviceIdType.MESH,
                    )
                )
        return made

    def sending(k):
        d, way = divmod(k, 2)
        return place[d] < count[d] - 1 if way == 0 else place[d] > 0

    def receiving(k):
        d, way = divmod(k, 2)
        return place[d] > 0 if way == 0 else place[d] < count[d] - 1

    def neighbours(step, d, f, a):
        tile = tr[d, f, 8 * a : 8 * a + 8, :]
        if d == 0:
            before = unpack_pairs(recv_x.at[step, 0], f) if a == 0 else tr[0, f, 8 * a - 8 : 8 * a, :]
            after = unpack_pairs(recv_x.at[step, 1], f) if a == 3 else tr[0, f, 8 * a + 8 : 8 * a + 16, :]
        elif d == 1:
            low = unpack_pairs(recv_y.at[step, 0], f)
            low = pltpu.roll(low, (8 - 2 * a) % 8, 0) if a else low
            before = jnp.where(sub < 2, low, pltpu.roll(tile, 2, 0))
            high = unpack_pairs(recv_y.at[step, 1], f)
            high = pltpu.roll(high, (6 - 2 * a) % 8, 0) if a < 3 else high
            after = jnp.where(sub >= 6, high, pltpu.roll(tile, 6, 0))
        else:
            low = recv_z[step, 0, f]
            high = recv_z[step, 1, f]
            if a % 2:
                low = pltpu.roll(low, 64, 1)
                high = pltpu.roll(high, 64, 1)
            if a < 2:
                low = pltpu.roll(low, 7, 0)
                high = pltpu.roll(high, 1, 0)
            before = jnp.where(even, low, pltpu.roll(tile, 1, 0))
            after = jnp.where(even, pltpu.roll(tile, 7, 0), high)
        return jnp.where(lo_lane, after, before)

    def corrections(step):
        sign = jnp.where(lo_lane, -1.0, 1.0)
        for d in range(3):
            for a in range(4):
                rows = slice(8 * a, 8 * a + 8)
                source = index[d, rows, :]
                w = [
                    jnp.take_along_axis(neighbours(step, d, f, a), source, axis=1) - tr[d, f, rows, :]
                    for f in range(FIELDS)
                ]
                inv, lam, mu, speed = [coef[i, rows, :] for i in range(4)]
                stiff = lam + 2.0 * mu
                if d == 0:
                    lam_v = lam * w[0]
                    flux = [inv * w[3], inv * w[6], inv * w[8], stiff * w[0], lam_v, lam_v,
                            mu * w[1], None, mu * w[2]]
                elif d == 1:
                    lam_v = lam * w[1]
                    flux = [inv * w[6], inv * w[4], inv * w[7], lam_v, stiff * w[1], lam_v,
                            mu * w[0], mu * w[2], None]
                else:
                    lam_v = lam * w[2]
                    flux = [inv * w[8], inv * w[7], inv * w[5], lam_v, lam_v, stiff * w[2],
                            None, mu * w[1], mu * w[0]]
                for f in range(FIELDS):
                    fixed = speed * w[f]
                    if flux[f] is not None:
                        fixed = fixed + sign * flux[f]
                    fixed = 0.5 * fixed
                    if d == 0:
                        cx[f, rows, :] = fixed
                    else:
                        tr[d, f, rows, :] = fixed
        for d in (1, 2):
            part = slice(128 * (d - 1), 128 * d)
            for f in range(FIELDS):
                ch[rows_of(f), part], cl[rows_of(f), part] = halves(tr[d, f])

    def step_body(step, carry):
        set_operand(q)
        advance(True, SERIES[1], False)
        advance(False, SERIES[2], False)

        def higher(k, c):
            weight = jnp.where(k == 0, SERIES[3], jnp.where(k == 1, SERIES[4], SERIES[5]))
            advance(False, weight.astype(F32), True)
            return c

        lax.fori_loop(0, 3, higher, 0)
        set_operand(acc)
        faces = dot(xh[...], pick[...]) + dot(xl[...], pick[...])
        for f in range(FIELDS):
            lower = acc[f, :, 0:128]
            upper = acc[f, :, 384:512]
            tr[0, f] = jnp.where(lane < 64, lower, upper)
            tr[1, f] = faces[rows_of(f), 0:128]
            tr[2, f] = faces[rows_of(f), 128:256]
        pack_pairs(lambda f: tr[0, f, 24:32, :], True, send_x.at[0])
        pack_pairs(lambda f: tr[0, f, 0:8, :], False, send_x.at[1])
        pack_pairs(lambda f: pack_rows_y(f, 6), True, send_y.at[0])
        pack_pairs(lambda f: pack_rows_y(f, 0), False, send_y.at[1])
        for f in range(FIELDS):
            send_z[0, f] = pack_z(f, True)
            send_z[1, f] = pack_z(f, False)

        @pl.when(step == 0)
        def _():
            pl.semaphore_wait(barrier, 6)

        made = copies(step)
        for k in range(6):

            @pl.when(sending(k))
            def _(k=k):
                made[k].start()

        derive()
        for k in range(6):

            @pl.when(receiving(k))
            def _(k=k):
                made[k].wait_recv()

        corrections(step)
        for j in range(4):
            part = slice(128 * j, 128 * (j + 1))
            for f, rate in enumerate(rates(part)):
                lifted = dot(ch[rows_of(f), :], lift[:, part]) + dot(cl[rows_of(f), :], lift[:, part])
                if j == 0:
                    lifted = lifted + jnp.where(lane < 64, cx[f], 0.0)
                if j == 3:
                    lifted = lifted + jnp.where(lane < 64, 0.0, cx[f])
                q[f, :, part] = q[f, :, part] + DT_STEP * (rate + LIFT_COEF * lifted)
        for k in range(6):

            @pl.when(sending(k))
            def _(k=k):
                made[k].wait_send()

        return carry

    lax.fori_loop(0, STEPS, step_body, 0)
    gather_out = (by_element[:, 10:11].astype(I32) == iota(square, 1)).astype(BF16)
    for f in range(FIELDS):
        a, b, c = thirds(q[f])
        out[f] = dot(gather_out, a) + dot(gather_out, b) + dot(gather_out, c)


def shards(
    wavefield, deriv_ops, density, lame_first, shear_modulus, high_order, element_cell, face_orient
):
    wave = jnp.swapaxes(wavefield[0, 0, 0], 0, 1)
    row = (1, ELEMENTS)
    vmem = pl.BlockSpec(memory_space=pltpu.VMEM)
    field = (FIELDS, ELEMENTS, NODES)
    total = FIELDS * ELEMENTS
    result = pl.pallas_call(
        kernel,
        out_shape=jax.ShapeDtypeStruct(field, F32),
        in_specs=[vmem, pl.BlockSpec(memory_space=pl.ANY)] + [vmem] * 6,
        out_specs=vmem,
        scratch_shapes=[
            pltpu.VMEM((3, NODES, NODES), F32),
            pltpu.VMEM((3, NODES, NODES), BF16),
            pltpu.VMEM((3, NODES, NODES), BF16),
            pltpu.VMEM((16, ELEMENTS), F32),
            pltpu.VMEM((4, ELEMENTS, 128), F32),
            pltpu.VMEM((ELEMENTS, 128), F32),
            pltpu.VMEM((3, ELEMENTS, 128), I32),
            pltpu.VMEM(field, F32),
            pltpu.VMEM(field, F32),
            pltpu.VMEM((total, NODES), BF16),
            pltpu.VMEM((total, NODES), BF16),
            pltpu.VMEM((3, 6 * ELEMENTS, NODES), F32),
            pltpu.VMEM((NODES, 256), BF16),
            pltpu.VMEM((256, NODES), BF16),
            pltpu.VMEM((3, FIELDS, ELEMENTS, 128), F32),
            pltpu.VMEM((total, 256), BF16),
            pltpu.VMEM((total, 256), BF16),
            pltpu.VMEM((FIELDS, ELEMENTS, 128), F32),
            pltpu.VMEM((2, 5, 8, 128), F32),
            pltpu.VMEM((2, 5, 8, 128), F32),
            pltpu.VMEM((2, FIELDS, 8, 128), F32),
            pltpu.VMEM((STEPS, 2, 5, 8, 128), F32),
            pltpu.VMEM((STEPS, 2, 5, 8, 128), F32),
            pltpu.VMEM((STEPS, 2, FIELDS, 8, 128), F32),
            pltpu.SemaphoreType.DMA((3,)),
            pltpu.SemaphoreType.DMA((STEPS, 6)),
            pltpu.SemaphoreType.DMA((STEPS, 6)),
        ],
        compiler_params=pltpu.CompilerParams(
            collective_id=0, has_side_effects=True, vmem_limit_bytes=60 * 1024 * 1024
        ),
        name="elastic_steps",
    )(
        wave,
        deriv_ops,
        density.reshape(row),
        lame_first.reshape(row),
        shear_modulus.reshape(row),
        high_order.reshape(row),
        element_cell.reshape(row),
        face_orient.reshape(6, ELEMENTS),
    )
    return jnp.swapaxes(result, 0, 1)[None, None, None]


def solution(mesh):
    row = P("gx", "gy", "ha", None)
    whole = P("gx", "gy", "ha", None, None, None)
    return jax.shard_map(
        shards,
        mesh=mesh,
        in_specs=(whole, P(), row, row, row, row, row, P("gx", "gy", "ha", None, None)),
        out_specs=whole,
        check_vma=False,
    )
```

profile of v0, /device:TPU:18, one launch (start us, length us, event | category | flops | bytes accessed | tf_op | source)
XLA Modules:
  0.0 34.8 jit_solution(2253582910110358082)
XLA Ops:
  0.0 1.3 %copy.11 = s32[1,1,1,6,32]{4,3,2,1,0:T(8,128)} copy(s32[1,1,1,6,32]{4,2,3,1,0:T(1,128)} %param.15) | data formatting | bytes 1536
  1.3 31.6 %elastic_steps.1 = f32[9,32,512]{2,1,0:T(8,128)} custom-call(f32[9,32,512]{2,1,0:T(8,128)} %bitcast.15, f32[3,512,512]{2,1,0:T(8,128)} %dops.1, f32[1,32]{1,0:T(1,128)} %bitcast.17, f32[1,32]{1,0:T(1,128)} %bitcast.18, f32[1,32]{1,0:T(1,128)} %bitcast.19, s32[1,32]{1,0:T(1,128)} %bitcast.20, s32[1,32]{1,0:T(1,128)} %bitcast.21, s32[6,32]{1,0:T(8,128)} %bitcast.16), custom_call_target="tpu_custom_call" | custom-call | tf_op jit(solution)/shard_map/elastic_steps/pallas_call | solution.py:380
  32.9 1.9 %copy.13 = f32[1,1,1,32,9,512]{5,3,4,2,1,0:T(8,128)} copy(f32[1,1,1,32,9,512]{5,3,4,2,1,0:T(8,128)} %bitcast.14) | data formatting | bytes 1179648
where the time goes:
time: 35 us; the launch traced here: 34.8 us
  Pallas kernels  31.6 us (90%)
  local copies, waits for them, and re-layouts  3.19 us (9%)
    pallas_call x1, Pallas kernels, shards(): pl.pallas_call(kernel, out_shape=jax.ShapeDtypeStruct(field, F32), in_spe...  31.6 us
    unnamed x2, local copies, waits for them, and re-layouts  3.19 us

commit v1 on v0

--- a/solution.py
+++ b/solution.py
@@ -8,6 +8,7 @@
 from jax.sharding import PartitionSpec as P
 
 ELEMENTS = 32
+HOT = 16
 FIELDS = 9
 NODES = 512
 STEPS = 2
@@ -59,9 +60,11 @@
 
 
 def kernel(
-    wave, dops, dens, lame, shear, hot, cell, orient, out,
-    wf, wh, wl, small, coef, flags, index, q, acc, xh, xl, deriv, pick, lift, tr, ch, cl, cx,
-    send_x, send_y, send_z, recv_x, recv_y, recv_z, load_sem, send_sem, recv_sem,
+    wave_in, dops, dens_in, lame_in, shear_in, hot_in, cell_in, orient_in, out,
+    wave, dens, lame, shear, hot, cell, orient,
+    wf, wh, wl, small, coef, index, q, acc, xh, xl, deriv, pick, lift, tr, ch, cl, cx,
+    hot_in_rows, hot_coef, hot_sum, yh, yl, hot_deriv, hot_sel,
+    send_x, send_y, send_z, recv_x, recv_y, recv_z, small_sem, load_sem, send_sem, recv_sem,
 ):
     barrier = pltpu.get_barrier_semaphore()
     place = [lax.axis_index(a) for a in MESH_AXES]
@@ -71,16 +74,30 @@
     for target in up + down:
         pl.semaphore_signal(barrier, 1, device_id=target, device_id_type=pl.DeviceIdType.MESH)
 
+    small_loads = [
+        pltpu.make_async_copy(source, dest, small_sem.at[i])
+        for i, (source, dest) in enumerate(
+            (
+                (cell_in, cell), (hot_in, hot), (dens_in, dens), (lame_in, lame),
+                (shear_in, shear), (orient_in, orient), (wave_in, wave),
+            )
+        )
+    ]
+    for load in small_loads:
+        load.start()
     loads = [pltpu.make_async_copy(dops.at[a], wf.at[a], load_sem.at[a]) for a in range(3)]
     for load in loads:
         load.start()
 
     small[...] = jnp.zeros_like(small)
+    for load in small_loads[:-1]:
+        load.wait()
     small[0:1, :] = dens[...]
     small[1:2, :] = lame[...]
     small[2:3, :] = shear[...]
     small[3:4, :] = hot[...].astype(F32)
-    small[4:10, :] = orient[...].astype(F32)
+    for i in range(6):
+        small[4 + i : 5 + i, :] = orient[i].astype(F32)
     small[10:11, :] = cell[...].astype(F32)
     square = (ELEMENTS, ELEMENTS)
     place_cell = (iota(square, 0) == jnp.broadcast_to(cell[...], square)).astype(F32)
@@ -95,7 +112,6 @@
     coef[1] = jnp.broadcast_to(lame_col, wide)
     coef[2] = jnp.broadcast_to(shear_col, wide)
     coef[3] = jnp.broadcast_to(jnp.sqrt((lame_col + 2.0 * shear_col) * inv_rho), wide)
-    flags[...] = jnp.broadcast_to(by_cell[:, 3:4], wide)
     lane = iota(wide, 1)
     p_pos = (lane // 8) % 8
     r_pos = lane % 8
@@ -109,7 +125,33 @@
         index[d] = node + jnp.where(lane < 64, 64, 0)
     pick[...] = (iota((NODES, 256), 0) == face_node(iota((NODES, 256), 1))).astype(BF16)
     lift[...] = (iota((256, NODES), 1) == face_node(iota((256, NODES), 0))).astype(BF16)
+    slots = (HOT, ELEMENTS)
+    flag_row = lax.dot_general(small[...], place_cell, NT, precision=HIGHEST)[3:4, :]
+    upto = (iota(square, 0) <= iota(square, 1)).astype(F32)
+    rank_row = lax.dot_general(
+        jnp.broadcast_to(flag_row, (8, ELEMENTS)), upto, (((1,), (0,)), ((), ())), precision=HIGHEST
+    )[0:1, :].astype(I32)
+    chosen = (iota(slots, 0) + 1 == jnp.broadcast_to(rank_row, slots)) & (
+        jnp.broadcast_to(flag_row, slots) > 0.5
+    )
+    select = chosen.astype(F32)
+    hot_sel[...] = select.astype(BF16)
+    of_slot = lax.dot_general(select, by_cell, (((1,), (0,)), ((), ())), precision=HIGHEST)
+    filled = of_slot[:, 0:1] > 0.0
+    hot_coef[0] = jnp.broadcast_to(
+        jnp.where(filled, 1.0 / jnp.where(filled, of_slot[:, 0:1], 1.0), 0.0), (HOT, 128)
+    )
+    hot_coef[1] = jnp.broadcast_to(of_slot[:, 1:2], (HOT, 128))
+    hot_coef[2] = jnp.broadcast_to(of_slot[:, 2:3], (HOT, 128))
+    slot_col = iota((ELEMENTS, HOT), 1) + 1
+    below = (iota(square, 1) <= iota(square, 0)).astype(F32)
+    rank_col = lax.dot_general(
+        below, jnp.broadcast_to(by_cell[:, 3:4], (ELEMENTS, 8)), (((1,), (0,)), ((), ())), precision=HIGHEST
+    )[:, 0:1]
+    back = (slot_col == rank_col.astype(I32)) & (by_cell[:, 3:4] > 0.5)
+    hot_in_rows[...] = back.astype(BF16)
     gather_in = place_cell.astype(BF16)
+    small_loads[-1].wait()
     for f in range(FIELDS):
         a, b, c = thirds(wave[f])
         q[f] = dot(gather_in, a) + dot(gather_in, b) + dot(gather_in, c)
@@ -144,11 +186,22 @@
             l = jnp.concatenate([xl[rows_of(f), :] for f in fields], axis=0)
             deriv[a] = dot(h, wh[a]) + dot(l, wh[a]) + dot(h, wl[a])
 
-    def rates(part):
-        x = [deriv[0, rows_of(i), part] for i in range(6)]
-        y = [deriv[1, rows_of(i), part] for i in range(6)]
-        z = [deriv[2, rows_of(i), part] for i in range(6)]
-        inv, lam, mu = coef[0], coef[1], coef[2]
+    def hot_rows(field):
+        return slice(HOT * field, HOT * (field + 1))
+
+    def derive_hot():
+        for a, fields in enumerate(AXIS_FIELDS):
+            h = [yh[hot_rows(f), :] for f in fields]
+            l = [yl[hot_rows(f), :] for f in fields]
+            both = dot(jnp.concatenate(h + l, axis=0), wh[a])
+            cross = dot(jnp.concatenate(h, axis=0), wl[a])
+            hot_deriv[a] = both[0 : 6 * HOT] + (both[6 * HOT :] + cross)
+
+    def rates(part, source=deriv, rows=rows_of, factors=coef):
+        x = [source[0, rows(i), part] for i in range(6)]
+        y = [source[1, rows(i), part] for i in range(6)]
+        z = [source[2, rows(i), part] for i in range(6)]
+        inv, lam, mu = factors[0], factors[1], factors[2]
         lam_div = lam * (x[0] + y[1] + z[2])
         mu2 = 2.0 * mu
         return [
@@ -163,14 +216,12 @@
             mu * (x[2] + z[0]),
         ]
 
-    def advance(first, weight, only_flagged):
+    def advance(first, weight):
         derive()
         for j in range(4):
             part = slice(128 * j, 128 * (j + 1))
             for f, rate in enumerate(rates(part)):
                 term = weight * rate
-                if only_flagged:
-                    term = jnp.where(flags[...] > 0.5, term, 0.0)
                 base = q if first else acc
                 acc[f, :, part] = base[f, :, part] + term
                 xh[rows_of(f), part], xl[rows_of(f), part] = halves(rate)
@@ -301,42 +352,57 @@
 
     def step_body(step, carry):
         set_operand(q)
-        advance(True, SERIES[1], False)
-        advance(False, SERIES[2], False)
+        advance(True, SERIES[1])
+        advance(False, SERIES[2])
+        for f in range(FIELDS):
+            yh[hot_rows(f), :] = dot(hot_sel[...], xh[rows_of(f), :]).astype(BF16)
+            yl[hot_rows(f), :] = dot(hot_sel[...], xl[rows_of(f), :]).astype(BF16)
+            hot_sum[f] = jnp.zeros_like(hot_sum[f])
 
         def higher(k, c):
-            weight = jnp.where(k == 0, SERIES[3], jnp.where(k == 1, SERIES[4], SERIES[5]))
-            advance(False, weight.astype(F32), True)
+            weight = jnp.where(k == 0, SERIES[3], jnp.where(k == 1, SERIES[4], SERIES[5])).astype(F32)
+            derive_hot()
+            for j in range(4):
+                part = slice(128 * j, 128 * (j + 1))
+                for f, rate in enumerate(rates(part, hot_deriv, hot_rows, hot_coef)):
+                    hot_sum[f, :, part] = hot_sum[f, :, part] + weight * rate
+                    yh[hot_rows(f), part], yl[hot_rows(f), part] = halves(rate)
             return c
 
         lax.fori_loop(0, 3, higher, 0)
-        set_operand(acc)
+        for f in range(FIELDS):
+            h, l = halves(hot_sum[f])
+            full = acc[f] + (dot(hot_in_rows[...], h) + dot(hot_in_rows[...], l))
+            acc[f] = full
+            xh[rows_of(f), :], xl[rows_of(f), :] = halves(full)
+            tr[0, f] = jnp.where(lane < 64, full[:, 0:128], full[:, 384:512])
+        pack_pairs(lambda f: tr[0, f, 24:32, :], True, send_x.at[0])
+        pack_pairs(lambda f: tr[0, f, 0:8, :], False, send_x.at[1])
+
+        @pl.when(step == 0)
+        def _():
+            pl.semaphore_wait(barrier, 6)
+
+        made = copies(step)
+
+        def send(first, last):
+            for k in range(first, last):
+
+                @pl.when(sending(k))
+                def _(k=k):
+                    made[k].start()
+
+        send(0, 2)
         faces = dot(xh[...], pick[...]) + dot(xl[...], pick[...])
         for f in range(FIELDS):
-            lower = acc[f, :, 0:128]
-            upper = acc[f, :, 384:512]
-            tr[0, f] = jnp.where(lane < 64, lower, upper)
             tr[1, f] = faces[rows_of(f), 0:128]
             tr[2, f] = faces[rows_of(f), 128:256]
-        pack_pairs(lambda f: tr[0, f, 24:32, :], True, send_x.at[0])
-        pack_pairs(lambda f: tr[0, f, 0:8, :], False, send_x.at[1])
         pack_pairs(lambda f: pack_rows_y(f, 6), True, send_y.at[0])
         pack_pairs(lambda f: pack_rows_y(f, 0), False, send_y.at[1])
         for f in range(FIELDS):
             send_z[0, f] = pack_z(f, True)
             send_z[1, f] = pack_z(f, False)
-
-        @pl.when(step == 0)
-        def _():
-            pl.semaphore_wait(barrier, 6)
-
-        made = copies(step)
-        for k in range(6):
-
-            @pl.when(sending(k))
-            def _(k=k):
-                made[k].start()
-
+        send(2, 6)
         derive()
         for k in range(6):
 
@@ -364,9 +430,13 @@
 
     lax.fori_loop(0, STEPS, step_body, 0)
     gather_out = (by_element[:, 10:11].astype(I32) == iota(square, 1)).astype(BF16)
+    stores = [pltpu.make_async_copy(acc.at[f], out.at[f], small_sem.at[f]) for f in range(FIELDS)]
     for f in range(FIELDS):
         a, b, c = thirds(q[f])
-        out[f] = dot(gather_out, a) + dot(gather_out, b) + dot(gather_out, c)
+        acc[f] = dot(gather_out, a) + dot(gather_out, b) + dot(gather_out, c)
+        stores[f].start()
+    for store in stores:
+        store.wait()
 
 
 def shards(
@@ -374,21 +444,27 @@
 ):
     wave = jnp.swapaxes(wavefield[0, 0, 0], 0, 1)
     row = (1, ELEMENTS)
-    vmem = pl.BlockSpec(memory_space=pltpu.VMEM)
+    any_space = pl.BlockSpec(memory_space=pl.ANY)
     field = (FIELDS, ELEMENTS, NODES)
     total = FIELDS * ELEMENTS
     result = pl.pallas_call(
         kernel,
         out_shape=jax.ShapeDtypeStruct(field, F32),
-        in_specs=[vmem, pl.BlockSpec(memory_space=pl.ANY)] + [vmem] * 6,
-        out_specs=vmem,
+        in_specs=[any_space] * 8,
+        out_specs=any_space,
         scratch_shapes=[
+            pltpu.VMEM(field, F32),
+            pltpu.VMEM(row, F32),
+            pltpu.VMEM(row, F32),
+            pltpu.VMEM(row, F32),
+            pltpu.VMEM(row, I32),
+            pltpu.VMEM(row, I32),
+            pltpu.VMEM((6, 1, ELEMENTS), I32),
             pltpu.VMEM((3, NODES, NODES), F32),
             pltpu.VMEM((3, NODES, NODES), BF16),
             pltpu.VMEM((3, NODES, NODES), BF16),
             pltpu.VMEM((16, ELEMENTS), F32),
             pltpu.VMEM((4, ELEMENTS, 128), F32),
-            pltpu.VMEM((ELEMENTS, 128), F32),
             pltpu.VMEM((3, ELEMENTS, 128), I32),
             pltpu.VMEM(field, F32),
             pltpu.VMEM(field, F32),
@@ -401,12 +477,20 @@
             pltpu.VMEM((total, 256), BF16),
             pltpu.VMEM((total, 256), BF16),
             pltpu.VMEM((FIELDS, ELEMENTS, 128), F32),
+            pltpu.VMEM((ELEMENTS, HOT), BF16),
+            pltpu.VMEM((3, HOT, 128), F32),
+            pltpu.VMEM((FIELDS, HOT, NODES), F32),
+            pltpu.VMEM((FIELDS * HOT, NODES), BF16),
+            pltpu.VMEM((FIELDS * HOT, NODES), BF16),
+            pltpu.VMEM((3, 6 * HOT, NODES), F32),
+            pltpu.VMEM((HOT, ELEMENTS), BF16),
             pltpu.VMEM((2, 5, 8, 128), F32),
             pltpu.VMEM((2, 5, 8, 128), F32),
             pltpu.VMEM((2, FIELDS, 8, 128), F32),
             pltpu.VMEM((STEPS, 2, 5, 8, 128), F32),
             pltpu.VMEM((STEPS, 2, 5, 8, 128), F32),
             pltpu.VMEM((STEPS, 2, FIELDS, 8, 128), F32),
+            pltpu.SemaphoreType.DMA((FIELDS,)),
             pltpu.SemaphoreType.DMA((3,)),
             pltpu.SemaphoreType.DMA((STEPS, 6)),
             pltpu.SemaphoreType.DMA((STEPS, 6)),
@@ -423,7 +507,7 @@
         shear_modulus.reshape(row),
         high_order.reshape(row),
         element_cell.reshape(row),
-        face_orient.reshape(6, ELEMENTS),
+        face_orient.reshape(6, 1, ELEMENTS),
     )
     return jnp.swapaxes(result, 0, 1)[None, None, None]
 

time: 35 us -> 30.8 us (0.88)
  the two profiles are of different devices: /device:TPU:18 before, /device:TPU:12 now
where the time goes in v1:
time: 30.8 us; the launch traced here: 30.6 us
  Pallas kernels  28.7 us (93%)
  local copies, waits for them, and re-layouts  1.92 us (6%)
    pallas_call x1, Pallas kernels, shards(): pl.pallas_call(kernel, out_shape=jax.ShapeDtypeStruct(field, F32), in_spe...  28.7 us
    unnamed x1, local copies, waits for them, and re-layouts  1.92 us

profile of v1, /device:TPU:12, one launch (start us, length us, event | category | flops | bytes accessed | tf_op | source)
XLA Modules:
  0.0 30.6 jit_solution(15329076256276671631)
XLA Ops:
  0.0 28.7 %elastic_steps.1 = f32[9,32,512]{2,1,0:T(8,128)} custom-call(f32[9,32,512]{2,1,0:T(8,128)} %bitcast.13, f32[3,512,512]{2,1,0:T(8,128)} %dops.1, f32[1,32]{1,0:T(1,128)} %bitcast.15, f32[1,32]{1,0:T(1,128)} %bitcast.16, f32[1,32]{1,0:T(1,128)} %bitcast.17, s32[1,32]{1,0:T(1,128)} %bitcast.18, s32[1,32]{1,0:T(1,128)} %bitcast.19, s32[6,1,32]{2,1,0:T(1,128)} %bitcast.14), custom_call_target="tpu_custom_call" | custom-call | tf_op jit(solution)/shard_map/elastic_steps/pallas_call | solution.py:450
  28.7 1.9 %copy.10 = f32[1,1,1,32,9,512]{5,3,4,2,1,0:T(8,128)} copy(f32[1,1,1,32,9,512]{5,3,4,2,1,0:T(8,128)} %bitcast.12) | data formatting | bytes 1179648

commit v2 on v1

--- a/solution.py
+++ b/solution.py
@@ -59,10 +59,28 @@
     return jnp.where(face < 2, p * 64 + far * 8 + r, p * 64 + r * 8 + far)
 
 
+def restore(state, cell_in, out, cell, full, sems):
+    load = pltpu.make_async_copy(cell_in, cell, sems.at[0])
+    load.start()
+    load.wait()
+    square = (ELEMENTS, ELEMENTS)
+    same = (iota(square, 0) == iota(square, 1)).astype(BF16)
+    row = jnp.broadcast_to(cell[...], (8, ELEMENTS)).astype(BF16)
+    column = lax.dot_general(same, row, NT, preferred_element_type=F32)[:, 0:1].astype(I32)
+    gather_out = (column == iota(square, 1)).astype(BF16)
+    stores = [pltpu.make_async_copy(full.at[f], out.at[f], sems.at[f]) for f in range(FIELDS)]
+    for f in range(FIELDS):
+        a, b, c = thirds(state[f])
+        full[f] = dot(gather_out, a) + dot(gather_out, b) + dot(gather_out, c)
+        stores[f].start()
+    for store in stores:
+        store.wait()
+
+
 def kernel(
-    wave_in, dops, dens_in, lame_in, shear_in, hot_in, cell_in, orient_in, out,
+    wave_in, dops, dens_in, lame_in, shear_in, hot_in, cell_in, orient_in, q,
     wave, dens, lame, shear, hot, cell, orient,
-    wf, wh, wl, small, coef, index, q, acc, xh, xl, deriv, pick, lift, tr, ch, cl, cx,
+    wf, wh, wl, small, coef, index, acc, xh, xl, deriv, pick, lift, tr, ch, cl, cx, spread,
     hot_in_rows, hot_coef, hot_sum, yh, yl, hot_deriv, hot_sel,
     send_x, send_y, send_z, recv_x, recv_y, recv_z, small_sem, load_sem, send_sem, recv_sem,
 ):
@@ -71,8 +89,15 @@
     count = [lax.axis_size(a) for a in MESH_AXES]
     up = [{a: lax.rem(i + 1, n)} for a, i, n in zip(MESH_AXES, place, count)]
     down = [{a: lax.rem(i + n - 1, n)} for a, i, n in zip(MESH_AXES, place, count)]
-    for target in up + down:
-        pl.semaphore_signal(barrier, 1, device_id=target, device_id_type=pl.DeviceIdType.MESH)
+    arrivals = 0
+    for d in range(3):
+        for target, steps_left in ((up[d], count[d] - 1 - place[d]), (down[d], place[d])):
+
+            @pl.when(steps_left > 0)
+            def _(target=target):
+                pl.semaphore_signal(barrier, 1, device_id=target, device_id_type=pl.DeviceIdType.MESH)
+
+            arrivals = arrivals + lax.div(steps_left + count[d] - 1, count[d])
 
     small_loads = [
         pltpu.make_async_copy(source, dest, small_sem.at[i])
@@ -102,8 +127,6 @@
     square = (ELEMENTS, ELEMENTS)
     place_cell = (iota(square, 0) == jnp.broadcast_to(cell[...], square)).astype(F32)
     by_cell = lax.dot_general(place_cell, small[...], NT, precision=HIGHEST)
-    same = (iota(square, 0) == iota(square, 1)).astype(F32)
-    by_element = lax.dot_general(same, small[...], NT, precision=HIGHEST)
     wide = (ELEMENTS, 128)
     inv_rho = 1.0 / by_cell[:, 0:1]
     lame_col = by_cell[:, 1:2]
@@ -154,7 +177,9 @@
     small_loads[-1].wait()
     for f in range(FIELDS):
         a, b, c = thirds(wave[f])
-        q[f] = dot(gather_in, a) + dot(gather_in, b) + dot(gather_in, c)
+        full = dot(gather_in, a) + dot(gather_in, b) + dot(gather_in, c)
+        q[f] = full
+        xh[rows_of(f), :], xl[rows_of(f), :] = halves(full)
 
     for a in range(3):
         loads[a].wait()
@@ -175,10 +200,6 @@
             def _(recv=recv, slot=slot):
                 for s in range(STEPS):
                     recv[s, slot] = jnp.zeros_like(recv[s, slot])
-
-    def set_operand(source):
-        for f in range(FIELDS):
-            xh[rows_of(f), :], xl[rows_of(f), :] = halves(source[f])
 
     def derive():
         for a, fields in enumerate(AXIS_FIELDS):
@@ -312,46 +333,44 @@
             after = jnp.where(even, pltpu.roll(tile, 7, 0), high)
         return jnp.where(lo_lane, after, before)
 
-    def corrections(step):
+    def corrections(step, d):
         sign = jnp.where(lo_lane, -1.0, 1.0)
-        for d in range(3):
-            for a in range(4):
-                rows = slice(8 * a, 8 * a + 8)
-                source = index[d, rows, :]
-                w = [
-                    jnp.take_along_axis(neighbours(step, d, f, a), source, axis=1) - tr[d, f, rows, :]
-                    for f in range(FIELDS)
-                ]
-                inv, lam, mu, speed = [coef[i, rows, :] for i in range(4)]
-                stiff = lam + 2.0 * mu
+        for a in range(4):
+            rows = slice(8 * a, 8 * a + 8)
+            source = index[d, rows, :]
+            w = [
+                jnp.take_along_axis(neighbours(step, d, f, a), source, axis=1) - tr[d, f, rows, :]
+                for f in range(FIELDS)
+            ]
+            inv, lam, mu, speed = [coef[i, rows, :] for i in range(4)]
+            stiff = lam + 2.0 * mu
+            if d == 0:
+                lam_v = lam * w[0]
+                flux = [inv * w[3], inv * w[6], inv * w[8], stiff * w[0], lam_v, lam_v,
+                        mu * w[1], None, mu * w[2]]
+            elif d == 1:
+                lam_v = lam * w[1]
+                flux = [inv * w[6], inv * w[4], inv * w[7], lam_v, stiff * w[1], lam_v,
+                        mu * w[0], mu * w[2], None]
+            else:
+                lam_v = lam * w[2]
+                flux = [inv * w[8], inv * w[7], inv * w[5], lam_v, lam_v, stiff * w[2],
+                        None, mu * w[1], mu * w[0]]
+            for f in range(FIELDS):
+                fixed = speed * w[f]
+                if flux[f] is not None:
+                    fixed = fixed + sign * flux[f]
+                fixed = 0.5 * fixed
                 if d == 0:
-                    lam_v = lam * w[0]
-                    flux = [inv * w[3], inv * w[6], inv * w[8], stiff * w[0], lam_v, lam_v,
-                            mu * w[1], None, mu * w[2]]
-                elif d == 1:
-                    lam_v = lam * w[1]
-                    flux = [inv * w[6], inv * w[4], inv * w[7], lam_v, stiff * w[1], lam_v,
-                            mu * w[0], mu * w[2], None]
+                    cx[f, rows, :] = fixed
                 else:
-                    lam_v = lam * w[2]
-                    flux = [inv * w[8], inv * w[7], inv * w[5], lam_v, lam_v, stiff * w[2],
-                            None, mu * w[1], mu * w[0]]
-                for f in range(FIELDS):
-                    fixed = speed * w[f]
-                    if flux[f] is not None:
-                        fixed = fixed + sign * flux[f]
-                    fixed = 0.5 * fixed
-                    if d == 0:
-                        cx[f, rows, :] = fixed
-                    else:
-                        tr[d, f, rows, :] = fixed
-        for d in (1, 2):
+                    tr[d, f, rows, :] = fixed
+        if d:
             part = slice(128 * (d - 1), 128 * d)
             for f in range(FIELDS):
                 ch[rows_of(f), part], cl[rows_of(f), part] = halves(tr[d, f])
 
     def step_body(step, carry):
-        set_operand(q)
         advance(True, SERIES[1])
         advance(False, SERIES[2])
         for f in range(FIELDS):
@@ -381,45 +400,64 @@
 
         @pl.when(step == 0)
         def _():
-            pl.semaphore_wait(barrier, 6)
+            pl.semaphore_wait(barrier, arrivals)
 
         made = copies(step)
 
-        def send(first, last):
-            for k in range(first, last):
+        def send(d):
+            for k in (2 * d, 2 * d + 1):
 
                 @pl.when(sending(k))
                 def _(k=k):
                     made[k].start()
 
-        send(0, 2)
+        send(0)
         faces = dot(xh[...], pick[...]) + dot(xl[...], pick[...])
         for f in range(FIELDS):
             tr[1, f] = faces[rows_of(f), 0:128]
             tr[2, f] = faces[rows_of(f), 128:256]
-        pack_pairs(lambda f: pack_rows_y(f, 6), True, send_y.at[0])
-        pack_pairs(lambda f: pack_rows_y(f, 0), False, send_y.at[1])
         for f in range(FIELDS):
             send_z[0, f] = pack_z(f, True)
             send_z[1, f] = pack_z(f, False)
-        send(2, 6)
+        send(2)
+        pack_pairs(lambda f: pack_rows_y(f, 6), True, send_y.at[0])
+        pack_pairs(lambda f: pack_rows_y(f, 0), False, send_y.at[1])
+        send(1)
         derive()
-        for k in range(6):
-
-            @pl.when(receiving(k))
-            def _(k=k):
-                made[k].wait_recv()
-
-        corrections(step)
         for j in range(4):
             part = slice(128 * j, 128 * (j + 1))
             for f, rate in enumerate(rates(part)):
-                lifted = dot(ch[rows_of(f), :], lift[:, part]) + dot(cl[rows_of(f), :], lift[:, part])
-                if j == 0:
-                    lifted = lifted + jnp.where(lane < 64, cx[f], 0.0)
-                if j == 3:
-                    lifted = lifted + jnp.where(lane < 64, 0.0, cx[f])
-                q[f, :, part] = q[f, :, part] + DT_STEP * (rate + LIFT_COEF * lifted)
+                acc[f, :, part] = q[f, :, part] + DT_STEP * rate
+
+        def receive(d):
+            for k in (2 * d, 2 * d + 1):
+
+                @pl.when(receiving(k))
+                def _(k=k):
+                    made[k].wait_recv()
+
+        receive(2)
+        corrections(step, 2)
+        receive(1)
+        corrections(step, 1)
+        spread[...] = dot(ch[...], lift[...]) + dot(cl[...], lift[...])
+        for f in range(FIELDS):
+            for j in range(4):
+                part = slice(128 * j, 128 * (j + 1))
+                full = acc[f, :, part] + (DT_STEP * LIFT_COEF) * spread[rows_of(f), part]
+                if j in (1, 2):
+                    q[f, :, part] = full
+                    xh[rows_of(f), part], xl[rows_of(f), part] = halves(full)
+                else:
+                    acc[f, :, part] = full
+        receive(0)
+        corrections(step, 0)
+        for f in range(FIELDS):
+            for j, mine in ((0, lane < 64), (3, lane >= 64)):
+                part = slice(128 * j, 128 * (j + 1))
+                full = acc[f, :, part] + jnp.where(mine, (DT_STEP * LIFT_COEF) * cx[f], 0.0)
+                q[f, :, part] = full
+                xh[rows_of(f), part], xl[rows_of(f), part] = halves(full)
         for k in range(6):
 
             @pl.when(sending(k))
@@ -429,14 +467,6 @@
         return carry
 
     lax.fori_loop(0, STEPS, step_body, 0)
-    gather_out = (by_element[:, 10:11].astype(I32) == iota(square, 1)).astype(BF16)
-    stores = [pltpu.make_async_copy(acc.at[f], out.at[f], small_sem.at[f]) for f in range(FIELDS)]
-    for f in range(FIELDS):
-        a, b, c = thirds(q[f])
-        acc[f] = dot(gather_out, a) + dot(gather_out, b) + dot(gather_out, c)
-        stores[f].start()
-    for store in stores:
-        store.wait()
 
 
 def shards(
@@ -444,14 +474,14 @@
 ):
     wave = jnp.swapaxes(wavefield[0, 0, 0], 0, 1)
     row = (1, ELEMENTS)
-    any_space = pl.BlockSpec(memory_space=pl.ANY)
+    any_space = pl.BlockSpec(memory_space=pltpu.HBM)
     field = (FIELDS, ELEMENTS, NODES)
     total = FIELDS * ELEMENTS
     result = pl.pallas_call(
         kernel,
         out_shape=jax.ShapeDtypeStruct(field, F32),
         in_specs=[any_space] * 8,
-        out_specs=any_space,
+        out_specs=pl.BlockSpec(memory_space=pltpu.VMEM),
         scratch_shapes=[
             pltpu.VMEM(field, F32),
             pltpu.VMEM(row, F32),
@@ -467,7 +497,6 @@
             pltpu.VMEM((4, ELEMENTS, 128), F32),
             pltpu.VMEM((3, ELEMENTS, 128), I32),
             pltpu.VMEM(field, F32),
-            pltpu.VMEM(field, F32),
             pltpu.VMEM((total, NODES), BF16),
             pltpu.VMEM((total, NODES), BF16),
             pltpu.VMEM((3, 6 * ELEMENTS, NODES), F32),
@@ -477,6 +506,7 @@
             pltpu.VMEM((total, 256), BF16),
             pltpu.VMEM((total, 256), BF16),
             pltpu.VMEM((FIELDS, ELEMENTS, 128), F32),
+            pltpu.VMEM((total, NODES), F32),
             pltpu.VMEM((ELEMENTS, HOT), BF16),
             pltpu.VMEM((3, HOT, 128), F32),
             pltpu.VMEM((FIELDS, HOT, NODES), F32),
@@ -496,19 +526,34 @@
             pltpu.SemaphoreType.DMA((STEPS, 6)),
         ],
         compiler_params=pltpu.CompilerParams(
-            collective_id=0, has_side_effects=True, vmem_limit_bytes=60 * 1024 * 1024
+            collective_id=0, has_side_effects=True, vmem_limit_bytes=24 * 1024 * 1024
         ),
         name="elastic_steps",
     )(
-        wave,
-        deriv_ops,
-        density.reshape(row),
-        lame_first.reshape(row),
-        shear_modulus.reshape(row),
-        high_order.reshape(row),
-        element_cell.reshape(row),
-        face_orient.reshape(6, 1, ELEMENTS),
+        *(
+            pltpu.with_memory_space_constraint(x, pltpu.HBM)
+            for x in (
+                wave,
+                deriv_ops,
+                density.reshape(row),
+                lame_first.reshape(row),
+                shear_modulus.reshape(row),
+                high_order.reshape(row),
+                element_cell.reshape(row),
+                face_orient.reshape(6, 1, ELEMENTS),
+            )
+        ),
     )
+    vmem = pl.BlockSpec(memory_space=pltpu.VMEM)
+    result = pl.pallas_call(
+        restore,
+        out_shape=jax.ShapeDtypeStruct(field, F32),
+        in_specs=[vmem, any_space],
+        out_specs=any_space,
+        scratch_shapes=[pltpu.VMEM(row, I32), pltpu.VMEM(field, F32), pltpu.SemaphoreType.DMA((FIELDS,))],
+        compiler_params=pltpu.CompilerParams(vmem_limit_bytes=8 * 1024 * 1024),
+        name="restore",
+    )(result, element_cell.reshape(row))
     return jnp.swapaxes(result, 0, 1)[None, None, None]
 
 

time: 30.8 us -> 26.8 us (0.87)
  the two profiles are of different devices: /device:TPU:12 before, /device:TPU:100 now
where the time goes in v2:
time: 26.8 us
  Pallas kernels  26.8 us (100%)
    pallas_call x1, Pallas kernels, shards(): pl.pallas_call(kernel, out_shape=jax.ShapeDtypeStruct(field, F32), in_spe...  25.5 us
    pallas_call x1, Pallas kernels, shards(): pl.pallas_call(restore, out_shape=jax.ShapeDtypeStruct(field, F32), in_sp...  1.29 us

profile of v2, /device:TPU:100, one launch (start us, length us, event | category | flops | bytes accessed | tf_op | source)
XLA Modules:
  0.0 26.8 jit_solution(4958140440391844687)
XLA Ops:
  0.0 0.0 copy-start
  0.0 25.5 %elastic_steps.1.state = f32[9,32,512]{2,1,0:T(8,128)S(1)} custom-call(f32[9,32,512]{2,1,0:T(8,128)} %bitcast.14, f32[3,512,512]{2,1,0:T(8,128)} %dops.1, f32[1,32]{1,0:T(1,128)} %bitcast.16, f32[1,32]{1,0:T(1,128)} %bitcast.17, f32[1,32]{1,0:T(1,128)} %bitcast.18, s32[1,32]{1,0:T(1,128)} %bitcast.19, s32[1,32]{1,0:T(1,128)} %bitcast.12, s32[6,1,32]{2,1,0:T(1,128)} %bitcast.15), custom_call_target="tpu_custom_call" | custom-call | tf_op jit(solution)/shard_map/elastic_steps/pallas_call | solution.py:480
  25.5 0.0 copy-done
  25.5 1.3 %restore.1 = f32[9,32,512]{2,1,0:T(8,128)} custom-call(f32[9,32,512]{2,1,0:T(8,128)S(1)} %elastic_steps.1.state, s32[1,32]{1,0:T(1,128)S(1)} %bitcast.13), custom_call_target="tpu_custom_call" | custom-call | tf_op jit(solution)/shard_map/restore/pallas_call | solution.py:548
Async XLA Ops:
  0.0 25.5 %copy-start = (s32[1,1,1,32]{3,2,1,0:T(1,128)S(1)}, s32[1,1,1,32]{3,2,1,0:T(1,128)}, u32[]{:S(2)}) copy-start(s32[1,1,1,32]{3,2,1,0:T(1,128)} %param.14) | copy-start | bytes 388

commit v3 on v2

--- a/solution.py
+++ b/solution.py
@@ -59,16 +59,9 @@
     return jnp.where(face < 2, p * 64 + far * 8 + r, p * 64 + r * 8 + far)
 
 
-def restore(state, cell_in, out, cell, full, sems):
-    load = pltpu.make_async_copy(cell_in, cell, sems.at[0])
-    load.start()
-    load.wait()
-    square = (ELEMENTS, ELEMENTS)
-    same = (iota(square, 0) == iota(square, 1)).astype(BF16)
-    row = jnp.broadcast_to(cell[...], (8, ELEMENTS)).astype(BF16)
-    column = lax.dot_general(same, row, NT, preferred_element_type=F32)[:, 0:1].astype(I32)
-    gather_out = (column == iota(square, 1)).astype(BF16)
+def restore(state, gather, out, full, sems):
     stores = [pltpu.make_async_copy(full.at[f], out.at[f], sems.at[f]) for f in range(FIELDS)]
+    gather_out = gather[...].astype(BF16)
     for f in range(FIELDS):
         a, b, c = thirds(state[f])
         full[f] = dot(gather_out, a) + dot(gather_out, b) + dot(gather_out, c)
@@ -78,7 +71,7 @@
 
 
 def kernel(
-    wave_in, dops, dens_in, lame_in, shear_in, hot_in, cell_in, orient_in, q,
+    wave_in, dops, dens_in, lame_in, shear_in, hot_in, cell_in, orient_in, q, gather_out,
     wave, dens, lame, shear, hot, cell, orient,
     wf, wh, wl, small, coef, index, acc, xh, xl, deriv, pick, lift, tr, ch, cl, cx, spread,
     hot_in_rows, hot_coef, hot_sum, yh, yl, hot_deriv, hot_sel,
@@ -89,16 +82,6 @@
     count = [lax.axis_size(a) for a in MESH_AXES]
     up = [{a: lax.rem(i + 1, n)} for a, i, n in zip(MESH_AXES, place, count)]
     down = [{a: lax.rem(i + n - 1, n)} for a, i, n in zip(MESH_AXES, place, count)]
-    arrivals = 0
-    for d in range(3):
-        for target, steps_left in ((up[d], count[d] - 1 - place[d]), (down[d], place[d])):
-
-            @pl.when(steps_left > 0)
-            def _(target=target):
-                pl.semaphore_signal(barrier, 1, device_id=target, device_id_type=pl.DeviceIdType.MESH)
-
-            arrivals = arrivals + lax.div(steps_left + count[d] - 1, count[d])
-
     small_loads = [
         pltpu.make_async_copy(source, dest, small_sem.at[i])
         for i, (source, dest) in enumerate(
@@ -114,6 +97,33 @@
     for load in loads:
         load.start()
 
+    arrivals = 0
+    for d in range(3):
+        for target, steps_left in ((up[d], count[d] - 1 - place[d]), (down[d], place[d])):
+
+            @pl.when(steps_left > 0)
+            def _(target=target):
+                pl.semaphore_signal(barrier, 1, device_id=target, device_id_type=pl.DeviceIdType.MESH)
+
+            arrivals = arrivals + lax.div(steps_left + count[d] - 1, count[d])
+
+    pick[...] = (iota((NODES, 256), 0) == face_node(iota((NODES, 256), 1))).astype(BF16)
+    lift[...] = (iota((256, NODES), 1) == face_node(iota((256, NODES), 0))).astype(BF16)
+
+    for recv, at, n in zip((recv_x, recv_y, recv_z), place, count):
+        for edge, slot in ((0, 0), (n - 1, 1)):
+
+            @pl.when(at == edge)
+            def _(recv=recv, slot=slot):
+                for s in range(STEPS):
+                    recv[s, slot] = jnp.zeros_like(recv[s, slot])
+
+    def derive():
+        for a, fields in enumerate(AXIS_FIELDS):
+            h = jnp.concatenate([xh[rows_of(f), :] for f in fields], axis=0)
+            l = jnp.concatenate([xl[rows_of(f), :] for f in fields], axis=0)
+            deriv[a] = dot(h, wh[a]) + dot(l, wh[a]) + dot(h, wl[a])
+
     small[...] = jnp.zeros_like(small)
     for load in small_loads[:-1]:
         load.wait()
@@ -126,6 +136,10 @@
     small[10:11, :] = cell[...].astype(F32)
     square = (ELEMENTS, ELEMENTS)
     place_cell = (iota(square, 0) == jnp.broadcast_to(cell[...], square)).astype(F32)
+    same = (iota(square, 0) == iota(square, 1)).astype(BF16)
+    cell_row = jnp.broadcast_to(cell[...], (8, ELEMENTS)).astype(F32).astype(BF16)
+    cell_col = lax.dot_general(same, cell_row, NT, preferred_element_type=F32)[:, 0:1]
+    gather_out[...] = (cell_col.astype(I32) == iota(square, 1)).astype(F32)
     by_cell = lax.dot_general(place_cell, small[...], NT, precision=HIGHEST)
     wide = (ELEMENTS, 128)
     inv_rho = 1.0 / by_cell[:, 0:1]
@@ -146,8 +160,6 @@
         r_src = jnp.where((code & 2) != 0, 7 - r_pos, r_pos)
         node = jnp.where((code & 4) != 0, r_src * 8 + p_src, p_src * 8 + r_src)
         index[d] = node + jnp.where(lane < 64, 64, 0)
-    pick[...] = (iota((NODES, 256), 0) == face_node(iota((NODES, 256), 1))).astype(BF16)
-    lift[...] = (iota((256, NODES), 1) == face_node(iota((256, NODES), 0))).astype(BF16)
     slots = (HOT, ELEMENTS)
     flag_row = lax.dot_general(small[...], place_cell, NT, precision=HIGHEST)[3:4, :]
     upto = (iota(square, 0) <= iota(square, 1)).astype(F32)
@@ -192,20 +204,6 @@
             return carry
 
         lax.fori_loop(0, NODES // 64, split, 0)
-
-    for recv, at, n in zip((recv_x, recv_y, recv_z), place, count):
-        for edge, slot in ((0, 0), (n - 1, 1)):
-
-            @pl.when(at == edge)
-            def _(recv=recv, slot=slot):
-                for s in range(STEPS):
-                    recv[s, slot] = jnp.zeros_like(recv[s, slot])
-
-    def derive():
-        for a, fields in enumerate(AXIS_FIELDS):
-            h = jnp.concatenate([xh[rows_of(f), :] for f in fields], axis=0)
-            l = jnp.concatenate([xl[rows_of(f), :] for f in fields], axis=0)
-            deriv[a] = dot(h, wh[a]) + dot(l, wh[a]) + dot(h, wl[a])
 
     def hot_rows(field):
         return slice(HOT * field, HOT * (field + 1))
@@ -389,12 +387,21 @@
             return c
 
         lax.fori_loop(0, 3, higher, 0)
-        for f in range(FIELDS):
-            h, l = halves(hot_sum[f])
-            full = acc[f] + (dot(hot_in_rows[...], h) + dot(hot_in_rows[...], l))
-            acc[f] = full
-            xh[rows_of(f), :], xl[rows_of(f), :] = halves(full)
-            tr[0, f] = jnp.where(lane < 64, full[:, 0:128], full[:, 384:512])
+        def complete(f, parts):
+            extra = jnp.concatenate([hot_sum[f, :, part] for part in parts], axis=1)
+            h, l = halves(extra)
+            extra = dot(hot_in_rows[...], h) + dot(hot_in_rows[...], l)
+            ends = []
+            for i, part in enumerate(parts):
+                full = acc[f, :, part] + extra[:, 128 * i : 128 * (i + 1)]
+                acc[f, :, part] = full
+                xh[rows_of(f), part], xl[rows_of(f), part] = halves(full)
+                ends.append(full)
+            return ends
+
+        for f in range(FIELDS):
+            ends = complete(f, (slice(0, 128), slice(384, 512)))
+            tr[0, f] = jnp.where(lane < 64, ends[0], ends[1])
         pack_pairs(lambda f: tr[0, f, 24:32, :], True, send_x.at[0])
         pack_pairs(lambda f: tr[0, f, 0:8, :], False, send_x.at[1])
 
@@ -412,6 +419,8 @@
                     made[k].start()
 
         send(0)
+        for f in range(FIELDS):
+            complete(f, (slice(128, 256), slice(256, 384)))
         faces = dot(xh[...], pick[...]) + dot(xl[...], pick[...])
         for f in range(FIELDS):
             tr[1, f] = faces[rows_of(f), 0:128]
@@ -436,10 +445,10 @@
                 def _(k=k):
                     made[k].wait_recv()
 
+        receive(1)
+        corrections(step, 1)
         receive(2)
         corrections(step, 2)
-        receive(1)
-        corrections(step, 1)
         spread[...] = dot(ch[...], lift[...]) + dot(cl[...], lift[...])
         for f in range(FIELDS):
             for j in range(4):
@@ -474,14 +483,18 @@
 ):
     wave = jnp.swapaxes(wavefield[0, 0, 0], 0, 1)
     row = (1, ELEMENTS)
+    vmem = pl.BlockSpec(memory_space=pltpu.VMEM)
     any_space = pl.BlockSpec(memory_space=pltpu.HBM)
     field = (FIELDS, ELEMENTS, NODES)
     total = FIELDS * ELEMENTS
-    result = pl.pallas_call(
+    state = pl.pallas_call(
         kernel,
-        out_shape=jax.ShapeDtypeStruct(field, F32),
+        out_shape=(
+            jax.ShapeDtypeStruct(field, F32),
+            jax.ShapeDtypeStruct((ELEMENTS, ELEMENTS), F32),
+        ),
         in_specs=[any_space] * 8,
-        out_specs=pl.BlockSpec(memory_space=pltpu.VMEM),
+        out_specs=(vmem, vmem),
         scratch_shapes=[
             pltpu.VMEM(field, F32),
             pltpu.VMEM(row, F32),
@@ -544,16 +557,15 @@
             )
         ),
     )
-    vmem = pl.BlockSpec(memory_space=pltpu.VMEM)
     result = pl.pallas_call(
         restore,
         out_shape=jax.ShapeDtypeStruct(field, F32),
-        in_specs=[vmem, any_space],
+        in_specs=[vmem, vmem],
         out_specs=any_space,
-        scratch_shapes=[pltpu.VMEM(row, I32), pltpu.VMEM(field, F32), pltpu.SemaphoreType.DMA((FIELDS,))],
+        scratch_shapes=[pltpu.VMEM(field, F32), pltpu.SemaphoreType.DMA((FIELDS,))],
         compiler_params=pltpu.CompilerParams(vmem_limit_bytes=8 * 1024 * 1024),
         name="restore",
-    )(result, element_cell.reshape(row))
+    )(*state)
     return jnp.swapaxes(result, 0, 1)[None, None, None]
 
 

time: 26.8 us -> 26.1 us (0.974)
  Pallas kernels: 26.8 us -> 26.1 us
    pallas_call x1, Pallas kernels: 25.5 us -> 25 us  [shards(): pl.pallas_call(kernel, out_shape=(jax.ShapeDtypeStruct(field, F32), jax.S...]
where the time goes in v3:
time: 26.1 us
  Pallas kernels  26.1 us (100%)
    pallas_call x1, Pallas kernels, shards(): pl.pallas_call(kernel, out_shape=(jax.ShapeDtypeStruct(field, F32), jax.S...  25 us
    pallas_call x1, Pallas kernels, shards(): pl.pallas_call(restore, out_shape=jax.ShapeDtypeStruct(field, F32), in_sp...  1.1 us

profile of v3, /device:TPU:100, one launch (start us, length us, event | category | flops | bytes accessed | tf_op | source)
XLA Modules:
  0.0 26.1 jit_solution(11489396988524798045)
XLA Ops:
  0.0 25.0 %elastic_steps.1 = (f32[9,32,512]{2,1,0:T(8,128)S(1)}, f32[32,32]{1,0:T(8,128)S(1)}) custom-call(f32[9,32,512]{2,1,0:T(8,128)} %bitcast.12, f32[3,512,512]{2,1,0:T(8,128)} %dops.1, f32[1,32]{1,0:T(1,128)} %bitcast.14, f32[1,32]{1,0:T(1,128)} %bitcast.15, f32[1,32]{1,0:T(1,128)} %bitcast.16, s32[1,32]{1,0:T(1,128)} %bitcast.17, s32[1,32]{1,0:T(1,128)} %bitcast.18, ...), custom_call_target="tpu_custom_call" | custom-call | tf_op jit(solution)/shard_map/elastic_steps/pallas_call | solution.py:490
  25.0 1.1 %restore.1 = f32[9,32,512]{2,1,0:T(8,128)} custom-call(f32[9,32,512]{2,1,0:T(8,128)S(1)} %get-tuple-element.7.state, f32[32,32]{1,0:T(8,128)S(1)} %get-tuple-element.8.gather), custom_call_target="tpu_custom_call" | custom-call | tf_op jit(solution)/shard_map/restore/pallas_call | solution.py:560

commit v4 on v3

--- a/solution.py
+++ b/solution.py
@@ -63,8 +63,7 @@
     stores = [pltpu.make_async_copy(full.at[f], out.at[f], sems.at[f]) for f in range(FIELDS)]
     gather_out = gather[...].astype(BF16)
     for f in range(FIELDS):
-        a, b, c = thirds(state[f])
-        full[f] = dot(gather_out, a) + dot(gather_out, b) + dot(gather_out, c)
+        full[f] = dot(gather_out, jnp.concatenate(thirds(state[f]), axis=0))
         stores[f].start()
     for store in stores:
         store.wait()
@@ -139,7 +138,8 @@
     same = (iota(square, 0) == iota(square, 1)).astype(BF16)
     cell_row = jnp.broadcast_to(cell[...], (8, ELEMENTS)).astype(F32).astype(BF16)
     cell_col = lax.dot_general(same, cell_row, NT, preferred_element_type=F32)[:, 0:1]
-    gather_out[...] = (cell_col.astype(I32) == iota(square, 1)).astype(F32)
+    triple = (ELEMENTS, 3 * ELEMENTS)
+    gather_out[...] = (cell_col.astype(I32) == iota(triple, 1) % ELEMENTS).astype(F32)
     by_cell = lax.dot_general(place_cell, small[...], NT, precision=HIGHEST)
     wide = (ELEMENTS, 128)
     inv_rho = 1.0 / by_cell[:, 0:1]
@@ -178,7 +178,7 @@
     )
     hot_coef[1] = jnp.broadcast_to(of_slot[:, 1:2], (HOT, 128))
     hot_coef[2] = jnp.broadcast_to(of_slot[:, 2:3], (HOT, 128))
-    slot_col = iota((ELEMENTS, HOT), 1) + 1
+    slot_col = iota((ELEMENTS, 2 * HOT), 1) % HOT + 1
     below = (iota(square, 1) <= iota(square, 0)).astype(F32)
     rank_col = lax.dot_general(
         below, jnp.broadcast_to(by_cell[:, 3:4], (ELEMENTS, 8)), (((1,), (0,)), ((), ())), precision=HIGHEST
@@ -389,8 +389,7 @@
         lax.fori_loop(0, 3, higher, 0)
         def complete(f, parts):
             extra = jnp.concatenate([hot_sum[f, :, part] for part in parts], axis=1)
-            h, l = halves(extra)
-            extra = dot(hot_in_rows[...], h) + dot(hot_in_rows[...], l)
+            extra = dot(hot_in_rows[...], jnp.concatenate(halves(extra), axis=0))
             ends = []
             for i, part in enumerate(parts):
                 full = acc[f, :, part] + extra[:, 128 * i : 128 * (i + 1)]
@@ -491,7 +490,7 @@
         kernel,
         out_shape=(
             jax.ShapeDtypeStruct(field, F32),
-            jax.ShapeDtypeStruct((ELEMENTS, ELEMENTS), F32),
+            jax.ShapeDtypeStruct((ELEMENTS, 3 * ELEMENTS), F32),
         ),
         in_specs=[any_space] * 8,
         out_specs=(vmem, vmem),
@@ -520,7 +519,7 @@
             pltpu.VMEM((total, 256), BF16),
             pltpu.VMEM((FIELDS, ELEMENTS, 128), F32),
             pltpu.VMEM((total, NODES), F32),
-            pltpu.VMEM((ELEMENTS, HOT), BF16),
+            pltpu.VMEM((ELEMENTS, 2 * HOT), BF16),
             pltpu.VMEM((3, HOT, 128), F32),
             pltpu.VMEM((FIELDS, HOT, NODES), F32),
             pltpu.VMEM((FIELDS * HOT, NODES), BF16),

time: 26.1 us -> 26 us (level)
  no operation moved by 1% of the time
where the time goes in v4:
time: 26 us; the launch traced here: 25.9 us
  Pallas kernels  25.9 us (100%)
    pallas_call x1, Pallas kernels, shards(): pl.pallas_call(kernel, out_shape=(jax.ShapeDtypeStruct(field, F32), jax.S...  24.9 us
    pallas_call x1, Pallas kernels, shards(): pl.pallas_call(restore, out_shape=jax.ShapeDtypeStruct(field, F32), in_sp...  1.03 us

profile of v4, /device:TPU:100, one launch (start us, length us, event | category | flops | bytes accessed | tf_op | source)
XLA Modules:
  0.0 25.9 jit_solution(8071497265892302550)
XLA Ops:
  0.0 24.9 %elastic_steps.1 = (f32[9,32,512]{2,1,0:T(8,128)S(1)}, f32[32,96]{1,0:T(8,128)S(1)}) custom-call(f32[9,32,512]{2,1,0:T(8,128)} %bitcast.12, f32[3,512,512]{2,1,0:T(8,128)} %dops.1, f32[1,32]{1,0:T(1,128)} %bitcast.14, f32[1,32]{1,0:T(1,128)} %bitcast.15, f32[1,32]{1,0:T(1,128)} %bitcast.16, s32[1,32]{1,0:T(1,128)} %bitcast.17, s32[1,32]{1,0:T(1,128)} %bitcast.18, ...), custom_call_target="tpu_custom_call" | custom-call | tf_op jit(solution)/shard_map/elastic_steps/pallas_call | solution.py:489
  24.9 1.0 %restore.1 = f32[9,32,512]{2,1,0:T(8,128)} custom-call(f32[9,32,512]{2,1,0:T(8,128)S(1)} %get-tuple-element.7.state, f32[32,96]{1,0:T(8,128)S(1)} %get-tuple-element.8.gather), custom_call_target="tpu_custom_call" | custom-call | tf_op jit(solution)/shard_map/restore/pallas_call | solution.py:559

commit v5 on v4

--- a/solution.py
+++ b/solution.py
@@ -185,11 +185,11 @@
     )[:, 0:1]
     back = (slot_col == rank_col.astype(I32)) & (by_cell[:, 3:4] > 0.5)
     hot_in_rows[...] = back.astype(BF16)
-    gather_in = place_cell.astype(BF16)
+    cells = jnp.concatenate([cell[...]] * 3, axis=1)
+    gather_in = (iota(triple, 0) == jnp.broadcast_to(cells, triple)).astype(BF16)
     small_loads[-1].wait()
     for f in range(FIELDS):
-        a, b, c = thirds(wave[f])
-        full = dot(gather_in, a) + dot(gather_in, b) + dot(gather_in, c)
+        full = dot(gather_in, jnp.concatenate(thirds(wave[f]), axis=0))
         q[f] = full
         xh[rows_of(f), :], xl[rows_of(f), :] = halves(full)
 
@@ -208,13 +208,20 @@
     def hot_rows(field):
         return slice(HOT * field, HOT * (field + 1))
 
-    def derive_hot():
+    def derive_hot(parts=(slice(0, NODES),)):
         for a, fields in enumerate(AXIS_FIELDS):
             h = [yh[hot_rows(f), :] for f in fields]
             l = [yl[hot_rows(f), :] for f in fields]
-            both = dot(jnp.concatenate(h + l, axis=0), wh[a])
-            cross = dot(jnp.concatenate(h, axis=0), wl[a])
-            hot_deriv[a] = both[0 : 6 * HOT] + (both[6 * HOT :] + cross)
+            right = jnp.concatenate([wh[a, :, part] for part in parts], axis=1)
+            both = dot(jnp.concatenate(h + l, axis=0), right)
+            right = jnp.concatenate([wl[a, :, part] for part in parts], axis=1)
+            cross = dot(jnp.concatenate(h, axis=0), right)
+            total = both[0 : 6 * HOT] + (both[6 * HOT :] + cross)
+            at = 0
+            for part in parts:
+                width = part.stop - part.start
+                hot_deriv[a, :, part] = total[:, at : at + width]
+                at += width
 
     def rates(part, source=deriv, rows=rows_of, factors=coef):
         x = [source[0, rows(i), part] for i in range(6)]
@@ -377,7 +384,7 @@
             hot_sum[f] = jnp.zeros_like(hot_sum[f])
 
         def higher(k, c):
-            weight = jnp.where(k == 0, SERIES[3], jnp.where(k == 1, SERIES[4], SERIES[5])).astype(F32)
+            weight = jnp.where(k == 0, SERIES[3], SERIES[4]).astype(F32)
             derive_hot()
             for j in range(4):
                 part = slice(128 * j, 128 * (j + 1))
@@ -386,7 +393,17 @@
                     yh[hot_rows(f), part], yl[hot_rows(f), part] = halves(rate)
             return c
 
-        lax.fori_loop(0, 3, higher, 0)
+        lax.fori_loop(0, 2, higher, 0)
+
+        def last_order(parts):
+            derive_hot(parts)
+            for part in parts:
+                for f, rate in enumerate(rates(part, hot_deriv, hot_rows, hot_coef)):
+                    hot_sum[f, :, part] = hot_sum[f, :, part] + SERIES[5] * rate
+
+        outer = (slice(0, 128), slice(384, 512))
+        inner = (slice(128, 256), slice(256, 384))
+        last_order(outer)
         def complete(f, parts):
             extra = jnp.concatenate([hot_sum[f, :, part] for part in parts], axis=1)
             extra = dot(hot_in_rows[...], jnp.concatenate(halves(extra), axis=0))
@@ -399,7 +416,7 @@
             return ends
 
         for f in range(FIELDS):
-            ends = complete(f, (slice(0, 128), slice(384, 512)))
+            ends = complete(f, outer)
             tr[0, f] = jnp.where(lane < 64, ends[0], ends[1])
         pack_pairs(lambda f: tr[0, f, 24:32, :], True, send_x.at[0])
         pack_pairs(lambda f: tr[0, f, 0:8, :], False, send_x.at[1])
@@ -418,8 +435,9 @@
                     made[k].start()
 
         send(0)
-        for f in range(FIELDS):
-            complete(f, (slice(128, 256), slice(256, 384)))
+        last_order(inner)
+        for f in range(FIELDS):
+            complete(f, inner)
         faces = dot(xh[...], pick[...]) + dot(xl[...], pick[...])
         for f in range(FIELDS):
             tr[1, f] = faces[rows_of(f), 0:128]

time: 26 us -> 25.9 us (level)
  Pallas kernels: 25.9 us -> 25.6 us
    pallas_call x1, Pallas kernels: 24.9 us -> 24.6 us  [shards(): pl.pallas_call(kernel, out_shape=(jax.ShapeDtypeStruct(field, F32), jax.S...]
where the time goes in v5:
time: 25.9 us; the launch traced here: 25.6 us
  Pallas kernels  25.6 us (99%)
    pallas_call x1, Pallas kernels, shards(): pl.pallas_call(kernel, out_shape=(jax.ShapeDtypeStruct(field, F32), jax.S...  24.6 us
    pallas_call x1, Pallas kernels, shards(): pl.pallas_call(restore, out_shape=jax.ShapeDtypeStruct(field, F32), in_sp...  1.03 us

profile of v5, /device:TPU:100, one launch (start us, length us, event | category | flops | bytes accessed | tf_op | source)
XLA Modules:
  0.0 25.6 jit_solution(11471711867953700022)
XLA Ops:
  0.0 24.6 %elastic_steps.1 = (f32[9,32,512]{2,1,0:T(8,128)S(1)}, f32[32,96]{1,0:T(8,128)S(1)}) custom-call(f32[9,32,512]{2,1,0:T(8,128)} %bitcast.12, f32[3,512,512]{2,1,0:T(8,128)} %dops.1, f32[1,32]{1,0:T(1,128)} %bitcast.14, f32[1,32]{1,0:T(1,128)} %bitcast.15, f32[1,32]{1,0:T(1,128)} %bitcast.16, s32[1,32]{1,0:T(1,128)} %bitcast.17, s32[1,32]{1,0:T(1,128)} %bitcast.18, ...), custom_call_target="tpu_custom_call" | custom-call | tf_op jit(solution)/shard_map/elastic_steps/pallas_call | solution.py:507
  24.6 1.0 %restore.1 = f32[9,32,512]{2,1,0:T(8,128)} custom-call(f32[9,32,512]{2,1,0:T(8,128)S(1)} %get-tuple-element.7.state, f32[32,96]{1,0:T(8,128)S(1)} %get-tuple-element.8.gather), custom_call_target="tpu_custom_call" | custom-call | tf_op jit(solution)/shard_map/restore/pallas_call | solution.py:577

commit v6 on v5

--- a/solution.py
+++ b/solution.py
@@ -393,6 +393,10 @@
                     yh[hot_rows(f), part], yl[hot_rows(f), part] = halves(rate)
             return c
 
+        @pl.when(step == 0)
+        def _():
+            pl.semaphore_wait(barrier, arrivals)
+
         lax.fori_loop(0, 2, higher, 0)
 
         def last_order(parts):
@@ -420,10 +424,6 @@
             tr[0, f] = jnp.where(lane < 64, ends[0], ends[1])
         pack_pairs(lambda f: tr[0, f, 24:32, :], True, send_x.at[0])
         pack_pairs(lambda f: tr[0, f, 0:8, :], False, send_x.at[1])
-
-        @pl.when(step == 0)
-        def _():
-            pl.semaphore_wait(barrier, arrivals)
 
         made = copies(step)
 

time: 25.9 us -> 25.9 us (level)
  no operation moved by 1% of the time
where the time goes in v6:
time: 25.9 us; the launch traced here: 25.6 us
  Pallas kernels  25.6 us (99%)
    pallas_call x1, Pallas kernels, shards(): pl.pallas_call(kernel, out_shape=(jax.ShapeDtypeStruct(field, F32), jax.S...  24.6 us
    pallas_call x1, Pallas kernels, shards(): pl.pallas_call(restore, out_shape=jax.ShapeDtypeStruct(field, F32), in_sp...  1.03 us

profile of v6, /device:TPU:100, one launch (start us, length us, event | category | flops | bytes accessed | tf_op | source)
XLA Modules:
  0.0 25.6 jit_solution(3975888333690006440)
XLA Ops:
  0.0 24.6 %elastic_steps.1 = (f32[9,32,512]{2,1,0:T(8,128)S(1)}, f32[32,96]{1,0:T(8,128)S(1)}) custom-call(f32[9,32,512]{2,1,0:T(8,128)} %bitcast.12, f32[3,512,512]{2,1,0:T(8,128)} %dops.1, f32[1,32]{1,0:T(1,128)} %bitcast.14, f32[1,32]{1,0:T(1,128)} %bitcast.15, f32[1,32]{1,0:T(1,128)} %bitcast.16, s32[1,32]{1,0:T(1,128)} %bitcast.17, s32[1,32]{1,0:T(1,128)} %bitcast.18, ...), custom_call_target="tpu_custom_call" | custom-call | tf_op jit(solution)/shard_map/elastic_steps/pallas_call | solution.py:507
  24.6 1.0 %restore.1 = f32[9,32,512]{2,1,0:T(8,128)} custom-call(f32[9,32,512]{2,1,0:T(8,128)S(1)} %get-tuple-element.7.state, f32[32,96]{1,0:T(8,128)S(1)} %get-tuple-element.8.gather), custom_call_target="tpu_custom_call" | custom-call | tf_op jit(solution)/shard_map/restore/pallas_call | solution.py:577
